TPU v7x, 32 devices: a whole 2x2x4 slice. The times are simulated.
32 devices in a mesh: streams: 8 (over z, x), tm: 4 (over y, core).
Axes of the slice: x: 2, y: 2, z: 4, core: 2. Of those that a mesh axis runs over, the one named last changes fastest.
Arguments:
- signal: float32 [2, 2097152], P(None, ('streams', 'tm')), parts along dimension 1, may hold values from -6 to 6
- coarse_taps: float32 [16, 64], replicated, may hold values from -1.5 to 1.5
- fine_taps: float32 [12, 512], replicated, may hold values from -1.8 to 1.8
Outputs:
- channelized: float32 [2, 64, 64, 512], P(None, 'tm', 'streams'), parts along dimension 2
There are 8 independent parts, one for each index of `streams`. A program takes and returns all parts, laid end to end along the dimension named above; an argument that names none is the same for every part. Nothing has to cross between parts.
All inputs are finite; a program needn't handle non-finite values.
Results may differ from a plain program's by a relative error of at most 0.00007.
Values sent between devices are 32-bit elements; how exact they have to be, the bound alone decides.
No kernel may reach another device: no remote copies, remote signals or barrier semaphores. Data moves between devices by JAX's collectives and lax.ppermute only.
A program may use at most 320 MiB of HBM per device.

v0:
```python
import math
import jax
import jax.numpy as jnp
from jax import lax
from jax.sharding import PartitionSpec as P

CHANNELS = 64
FINE = 512
TAPS = 16
FINE_TAPS = 12


def from_behind(array, axis, by):
    length = lax.axis_size(axis)
    pairs = [(i, i + by) for i in range(length) if 0 <= i + by < length]
    return lax.ppermute(array, axis, pairs)


def tables(points):
    counter = jnp.arange(points, dtype=jnp.int32)
    product = counter[:, None] * counter[None, :] % points
    angle = product.astype(jnp.float32) * (2.0 * math.pi / points)
    return (jnp.cos(angle), jnp.sin(angle))


def coarse_branches(extended, coarse_taps, length):
    row_count = length // (2 * CHANNELS)
    summed = jnp.zeros((2, row_count, 2 * CHANNELS), jnp.float32)
    for tap_index in range(TAPS):
        offset = (TAPS - 1 - tap_index) * CHANNELS
        segment = extended[:, offset : offset + length].reshape(2, row_count, 2 * CHANNELS)
        summed = summed + segment * jnp.tile(coarse_taps[tap_index], 2)
    return summed.reshape(2, length // CHANNELS, CHANNELS)


def coarse_spectrum(branches, cosine_rows, sine_rows):
    factor = 1.0 / math.sqrt(CHANNELS)
    highest = lax.Precision.HIGHEST
    real_part = (
        jnp.einsum("kp,tp->kt", cosine_rows, branches[0], precision=highest)
        + jnp.einsum("kp,tp->kt", sine_rows, branches[1], precision=highest)
    ) * factor
    imag_part = (
        jnp.einsum("kp,tp->kt", cosine_rows, branches[1], precision=highest)
        - jnp.einsum("kp,tp->kt", sine_rows, branches[0], precision=highest)
    ) * factor
    return jnp.stack([real_part, imag_part])


def fine_section(coarse, fine_taps):
    group_size = coarse.shape[1]
    fine_frames = coarse.shape[2] // FINE
    shaped = coarse.reshape(2, group_size, fine_frames, FINE)
    padded = jnp.pad(shaped, ((0, 0), (0, 0), (FINE_TAPS - 1, 0), (0, 0)))
    summed = jnp.zeros((2, group_size, fine_frames, FINE), jnp.float32)
    for tap_index in range(FINE_TAPS):
        offset = FINE_TAPS - 1 - tap_index
        summed = summed + fine_taps[tap_index] * padded[:, :, offset : offset + fine_frames, :]
    cosine_table, sine_table = tables(FINE)
    factor = 1.0 / math.sqrt(FINE)
    highest = lax.Precision.HIGHEST
    out_real = (
        jnp.matmul(summed[0], cosine_table, precision=highest)
        + jnp.matmul(summed[1], sine_table, precision=highest)
    ) * factor
    out_imag = (
        jnp.matmul(summed[1], cosine_table, precision=highest)
        - jnp.matmul(summed[0], sine_table, precision=highest)
    ) * factor
    return jnp.stack([out_real, out_imag])


def on_device(signal, coarse_taps, fine_taps):
    length = signal.shape[1]
    history = (TAPS - 1) * CHANNELS
    cosine_table, sine_table = tables(CHANNELS)
    previous = from_behind(signal[:, length - history :], "tm", 1)
    extended = jnp.concatenate([previous, signal], axis=1)
    branches = coarse_branches(extended, coarse_taps, length)
    coarse = lax.all_to_all(
        coarse_spectrum(branches, cosine_table, sine_table),
        "tm",
        split_axis=1,
        concat_axis=2,
        tiled=True,
    )
    return fine_section(coarse, fine_taps)


def solution(mesh):
    return jax.shard_map(
        on_device,
        mesh=mesh,
        in_specs=(P(None, ("streams", "tm")), P(), P()),
        out_specs=P(None, "tm", "streams", None),
        check_vma=False,
    )
```

profile of v0, /device:TPU:0, one launch (start us, length us, event | category | flops | bytes accessed | tf_op | source)
XLA Modules:
  0.0 54.4 jit_solution(16357406457331470736)
XLA Ops:
  0.0 0.8 %slice.180 = f32[2,960]{1,0:T(2,128)S(1)} slice(f32[2,65536]{1,0:T(2,128)} %param.3), slice={[0:2], [64576:65536]} | slice | bytes 15360 | tf_op jit(solution)/shard_map/slice | solution.py:77
  0.8 2.4 %collective-permute-start = (f32[2,960]{1,0:T(2,128)S(1)}, f32[2,960]{1,0:T(2,128)S(1)}, u32[]{:S(2)}, u32[]{:S(2)}) collective-permute-start(f32[2,960]{1,0:T(2,128)S(1)} %slice.180), channel_id=1, source_target_pairs={{0,1},{1,2},{2,3},{4,5},{5,6},{6,7},{8,9},{9,10},{10,11},{12,13},{... | collective-permute-start | bytes 23048 | tf_op jit(solution)/shard_map/ppermute | solution.py:16
  3.2 1.0 %slice_bitcast_fusion.21 = (f32[64]{0:T(128)S(1)}, f32[64]{0:T(128)S(1)}, f32[64]{0:T(128)S(1)}, f32[64]{0:T(128)S(1)}, f32[64]{0:T(128)S(1)}, /*index=5*/f32[64...) fusion(f32[16,64]{1,0:T(8,128)} %param.4), kind=kLoop, calls=%fused_computation.166 | loop fusion | bytes 8192 | tf_op jit(solution)/shard_map/tile | solution.py:32
  5.6 4.7 %fusion.23 = (f32[1,2,512,128]{3,1,2,0:T(2,128)S(1)}, f32[1,2,512,128]{3,1,2,0:T(2,128)S(1)}, f32[1,2,512,128]{3,1,2,0:T(2,128)S(1)}, f32[1,2,512,128]{3,1,2,0:T...) fusion(f32[2,960]{1,0:T(2,128)S(1)} %collective-permute-done, f32[2,65536]{1,0:T(2,128)} %param.3), kind=kLoop, calls=%fused_computation.51 | loop fusion | flops 786432 | bytes 3677696
  10.3 2.6 %fusion.35 = (f32[1,2,512,128]{3,1,2,0:T(2,128)S(1)}, f32[1,2,512,128]{3,1,2,0:T(2,128)S(1)}, f32[1,2,512,128]{3,1,2,0:T(2,128)S(1)}, f32[1,2,512,128]{3,1,2,0:T...) fusion(f32[2,960]{1,0:T(2,128)S(1)} %collective-permute-done, f32[2,65536]{1,0:T(2,128)S(1)} %copy-done), kind=kLoop, calls=%fused_computation.63 | loop fusion | flops 786432 | bytes 3677696
  12.9 1.3 %fusion.47 = (f32[1,2,512,128]{3,1,2,0:T(2,128)S(1)}, f32[1,2,512,128]{3,1,2,0:T(2,128)S(1)}, f32[1,2,512,128]{3,1,2,0:T(2,128)S(1)}) fusion(f32[2,960]{1,0:T(2,128)S(1)} %collective-permute-done, f32[2,65536]{1,0:T(2,128)S(1)} %copy-done), kind=kLoop, calls=%fused_computation.75 | loop fusion | flops 393216 | bytes 2104832
  14.2 0.6 %fusion.66 = f32[2,512,128]{2,1,0:T(8,128)S(1)} fusion(f32[1,2,512,128]{3,1,2,0:T(2,128)S(1)} %get-tuple-element.18, f32[1,2,512,128]{3,1,2,0:T(2,128)S(1)} %get-tuple-element.19, f32[1,2,512,128]{3,1,2,0:T(2,128)S(1)} %get-tuple-element.17, f32[1,2,512,128]{3,1,2,0:T(2,128)S(1)} %get-tuple-element.16, f32[1,2,512,128]{3,1,2,0:T(2,128)S(1)} %get-tuple-element.15, ...), kind=kLoop, calls=%fused_computation.95 | loop fusion | flops 4063232 | bytes 8921088 | tf_op jit(solution)/shard_map/add | solution.py:32
  14.8 0.1 squeeze.16
  15.0 0.8 %fusion.98 = f32[64,1024]{1,0:T(8,128)S(1)} fusion(f32[1024,64]{1,0:T(8,128)S(1)} %squeeze.16), kind=kOutput, calls=%fused_computation.146 | convolution fusion | flops 50388992 | bytes 524288 | tf_op jit(solution)/shard_map/kp,tp->kt/dot_general | solution.py:40
  15.8 0.2 squeeze.17
  15.9 0.8 %fusion.96 = f32[64,1024]{1,0:T(8,128)S(1)} fusion(f32[1024,64]{1,0:T(8,128)S(1)} %squeeze.17), kind=kOutput, calls=%fused_computation.145 | convolution fusion | flops 50388992 | bytes 524288 | tf_op jit(solution)/shard_map/kp,tp->kt/dot_general | solution.py:44
  16.7 0.8 %fusion.3 = f32[1,64,1024]{2,1,0:T(8,128)S(1)} fusion(f32[64,1024]{1,0:T(8,128)S(1)} %fusion.98, f32[1024,64]{1,0:T(8,128)S(1)} %squeeze.17), kind=kOutput, calls=%fused_computation.29 | convolution fusion | flops 50520064 | bytes 786432 | tf_op jit(solution)/shard_map/kp,tp->kt/dot_general | solution.py:41
  17.5 0.8 %fusion.1 = f32[1,64,1024]{2,1,0:T(8,128)S(1)} fusion(f32[64,1024]{1,0:T(8,128)S(1)} %fusion.96, f32[1024,64]{1,0:T(8,128)S(1)} %squeeze.16), kind=kOutput, calls=%fused_computation.26 | convolution fusion | flops 50520064 | bytes 786432 | tf_op jit(solution)/shard_map/kp,tp->kt/dot_general | solution.py:45
  18.4 1.2 %copy.6 = f32[2,64,1024]{2,0,1:T(2,128)} copy(f32[2,64,1024]{2,1,0:T(8,128)S(1)} %pad_maximum_fusion.1) | data formatting | bytes 1048576 | tf_op jit(solution)/shard_map/stack | solution.py:47
  19.6 4.5 %all-to-all-start = ((f32[2,64,1024]{2,0,1:T(2,128)}), f32[2,64,1024]{2,0,1:T(2,128)S(1)}, u32[]{:S(2)}, u32[]{:S(2)}) async-start(f32[2,64,1024]{2,0,1:T(2,128)} %copy.6), calls=%async_computation | async-start | bytes 1048576 | tf_op jit(solution)/shard_map/all_to_all | solution.py:80
  24.1 8.8 %all-to-all-done = f32[2,64,1024]{2,0,1:T(2,128)S(1)} async-done(((f32[2,64,1024]{2,0,1:T(2,128)}), f32[2,64,1024]{2,0,1:T(2,128)S(1)}, u32[]{:S(2)}, u32[]{:S(2)}) %all-to-all-start) | async-done | bytes 524320 | tf_op jit(solution)/shard_map/all_to_all | solution.py:80
  32.9 0.3 copy.41
  33.3 0.2 reshape.109
  33.5 0.6 %fusion.59 = f32[2,16,8,512]{3,2,1,0:T(8,128)S(1)} fusion(f32[2,16,8,512]{3,2,1,0:T(8,128)S(1)} %reshape.109, f32[512]{0:T(512)S(1)} %bitcast.214, f32[512]{0:T(512)S(1)} %bitcast.215, f32[512]{0:T(512)S(1)} %bitcast.205, f32[512]{0:T(512)S(1)} %bitcast.206, f32[512]{0:T(512)S(1)} %bitcast.207, f32[512]{0:T(512)S(1)} %bitcast.208, f32[512]{0:T(512)S(1)} %bitcast.209, ...), kind=kLoop, calls=%fused_computation.87 | loop fusion | flops 2490368 | bytes 1073152 | tf_op jit(solution)/shard_map/add | solution.py:58
  34.1 4.9 %fusion.15 = f32[16,8,512]{2,1,0:T(8,128)S(1)} fusion(f32[2,16,8,512]{3,2,1,0:T(8,128)S(1)} %fusion.59), kind=kOutput, calls=%fused_computation.43 | convolution fusion | flops 406323200 | bytes 524288 | tf_op jit(solution)/shard_map/dot_general | solution.py:63
  39.0 4.9 %fusion.13 = f32[16,8,512]{2,1,0:T(8,128)S(1)} fusion(f32[2,16,8,512]{3,2,1,0:T(8,128)S(1)} %fusion.59), kind=kOutput, calls=%fused_computation.41 | convolution fusion | flops 406323200 | bytes 524288 | tf_op jit(solution)/shard_map/dot_general | solution.py:67
  43.8 4.9 %fusion.7 = f32[1,16,8,512]{3,2,1,0:T(8,128)S(1)} fusion(f32[16,8,512]{2,1,0:T(8,128)S(1)} %fusion.15, f32[2,16,8,512]{3,2,1,0:T(8,128)S(1)} %fusion.59), kind=kOutput, calls=%fused_computation.35 | convolution fusion | flops 406454272 | bytes 786432 | tf_op jit(solution)/shard_map/dot_general | solution.py:64
  48.7 4.9 %fusion.5 = f32[1,16,8,512]{3,2,1,0:T(8,128)S(1)} fusion(f32[16,8,512]{2,1,0:T(8,128)S(1)} %fusion.13, f32[2,16,8,512]{3,2,1,0:T(8,128)S(1)} %fusion.59), kind=kOutput, calls=%fused_computation.32 | convolution fusion | flops 406454272 | bytes 786432 | tf_op jit(solution)/shard_map/dot_general | solution.py:68
  53.6 0.8 %pad_maximum_fusion.2 = f32[2,16,8,512]{3,2,1,0:T(8,128)} fusion(f32[1,16,8,512]{3,2,1,0:T(8,128)S(1)} %fusion.5, f32[1,16,8,512]{3,2,1,0:T(8,128)S(1)} %fusion.7), kind=kLoop, calls=%fused_computation.128 | loop fusion | flops 131072 | bytes 1048576 | tf_op jit(solution)/shard_map/stack | solution.py:70
  (40 shorter events, 1.5 us)
Async XLA Ops:
  0.8 4.8 %collective-permute-start = (f32[2,960]{1,0:T(2,128)S(1)}, f32[2,960]{1,0:T(2,128)S(1)}, u32[]{:S(2)}, u32[]{:S(2)}) collective-permute-start(f32[2,960]{1,0:T(2,128)S(1)} %slice.180), channel_id=1, source_target_pairs={{0,1},{1,2},{2,3},{4,5},{5,6},{6,7},{8,9},{9,10},{10,11},{12,13},{... | collective-permute-start | bytes 23048 | tf_op jit(solution)/shard_map/ppermute | solution.py:16
  5.6 4.7 %copy-start = (f32[2,65536]{1,0:T(2,128)S(1)}, f32[2,65536]{1,0:T(2,128)}, u32[]{:S(2)}) copy-start(f32[2,65536]{1,0:T(2,128)} %param.3) | copy-start | bytes 1572868
  19.6 4.5 %copy-start.1 = (f32[12,512]{1,0:T(8,128)S(1)}, f32[12,512]{1,0:T(8,128)}, u32[]{:S(2)}) copy-start(f32[12,512]{1,0:T(8,128)} %param.5) | copy-start | bytes 73732
  19.6 13.3 %all-to-all-start = ((f32[2,64,1024]{2,0,1:T(2,128)}), f32[2,64,1024]{2,0,1:T(2,128)S(1)}, u32[]{:S(2)}, u32[]{:S(2)}) async-start(f32[2,64,1024]{2,0,1:T(2,128)} %copy.6), calls=%async_computation | async-start | bytes 1048576 | tf_op jit(solution)/shard_map/all_to_all | solution.py:80
where the time goes:
time: 54.7 us; the launch traced here: 54.4 us
  matrix products  22.7 us (41%)
  other arithmetic  10.6 us (19%)
  waiting for transfers between devices  8.79 us (16%)
  starting transfers between devices  6.89 us (13%)
  local copies, waits for them, and re-layouts  5.27 us (10%)
    all_to_all x1, waiting for transfers between devices, on_device(): lax.all_to_all(coarse_spectrum(branches, cosine_table, sine_table), 'tm',...  8.79 us
    unnamed x3, other arithmetic  8.52 us
    dot_general x1, matrix products, fine_section(): jnp.matmul(summed[0], cosine_table, precision=highest)  4.87 us
    dot_general x1, matrix products, fine_section(): jnp.matmul(summed[1], cosine_table, precision=highest)  4.87 us
    dot_general x1, matrix products, fine_section(): jnp.matmul(summed[0], sine_table, precision=highest)  4.86 us
    dot_general x1, matrix products, fine_section(): jnp.matmul(summed[1], sine_table, precision=highest)  4.86 us
    all_to_all x1, starting transfers between devices, on_device(): lax.all_to_all(coarse_spectrum(branches, cosine_table, sine_table), 'tm',...  4.5 us
    ppermute x1, starting transfers between devices, from_behind(): return lax.ppermute(array, axis, pairs)  2.39 us
  transfers between devices with their start and end apart: 2, of which 1 were waited for; matrix products, arithmetic and copies ran while one was open for 4% of the time, Pallas kernels for 0%

commit v1 on v0

--- a/solution.py
+++ b/solution.py
@@ -8,6 +8,17 @@
 FINE = 512
 TAPS = 16
 FINE_TAPS = 12
+
+
+def split_up(x, dim, size):
+    before, after = (x.shape[:dim], x.shape[dim + 1 :])
+    return jnp.moveaxis(x.reshape(*before, size, -1, *after), dim, 0)
+
+
+def in_order(pieces, dim):
+    dims = list(pieces.shape[1:])
+    dims[dim] *= pieces.shape[0]
+    return jnp.moveaxis(pieces, 0, dim).reshape(dims)
 
 
 def from_behind(array, axis, by):
@@ -77,13 +88,15 @@
     previous = from_behind(signal[:, length - history :], "tm", 1)
     extended = jnp.concatenate([previous, signal], axis=1)
     branches = coarse_branches(extended, coarse_taps, length)
-    coarse = lax.all_to_all(
-        coarse_spectrum(branches, cosine_table, sine_table),
-        "tm",
-        split_axis=1,
-        concat_axis=2,
-        tiled=True,
-    )
+    x = coarse_spectrum(branches, cosine_table, sine_table)
+    count, here = (lax.axis_size("tm"), lax.axis_index("tm"))
+    blocks = split_up(x, 1, count)
+    outs = [blocks[here]]
+    for lap in range(1, count):
+        sent = blocks[here ^ lap]
+        outs.append(lax.ppermute(sent, "tm", [(i_2, i_2 ^ lap) for i_2 in range(count)]))
+    blocks = jnp.stack(outs)[here ^ jnp.arange(count)]
+    coarse = in_order(blocks, 2)
     return fine_section(coarse, fine_taps)
 
 

time: 54.7 us -> 52.4 us (0.958)
  waiting for transfers between devices: 8.79 us -> 5.95 us
  other arithmetic: 10.6 us -> 11.7 us
  local copies, waits for them, and re-layouts: 5.27 us -> 4.65 us
    all_to_all x1 -> x0, waiting for transfers between devices: 8.79 us -> none  [on_device(): lax.all_to_all(coarse_spectrum(branches, cosine_table, sine_table), 'tm',...]
    ppermute x0 -> x3, waiting for transfers between devices: none -> 5.94 us  [on_device(): lax.ppermute(sent, 'tm', [(i_2, i_2 ^ lap) for i_2 in range(count)])]
    all_to_all x1 -> x0, starting transfers between devices: 4.5 us -> none  [on_device(): lax.all_to_all(coarse_spectrum(branches, cosine_table, sine_table), 'tm',...]
    ppermute x0 -> x3, starting transfers between devices: none -> 4.12 us  [on_device(): lax.ppermute(sent, 'tm', [(i_2, i_2 ^ lap) for i_2 in range(count)])]
    slice x1, other arithmetic: 0.02 us -> 1.04 us  [fine_section(): fine_taps[tap_index] * padded[:, :, offset:offset + fine_frames, :]]
    another operation x1, local copies, waits for them, and re-layouts: 1.2 us -> 0.21 us  [fine_section(): shaped = coarse.reshape(2, group_size, fine_frames, FINE)]
    gather x0 -> x1, local copies, waits for them, and re-layouts: none -> 0.58 us  [on_device(): blocks = jnp.stack(outs)[here ^ jnp.arange(count)]]
  transfers between devices with their start and end apart: 2 -> 4, of which waited for: 1 -> 2; matrix products, arithmetic and copies ran while one was open for 4% -> 7% of each run, Pallas kernels for 0% -> 0%
where the time goes in v1:
time: 52.4 us; the launch traced here: 51.9 us
  matrix products  22.9 us (44%)
  other arithmetic  11.7 us (22%)
  starting transfers between devices  6.51 us (12%)
  waiting for transfers between devices  5.95 us (11%)
  local copies, waits for them, and re-layouts  4.65 us (9%)
    unnamed x3, other arithmetic  8.52 us
    ppermute x3, waiting for transfers between devices, on_device(): lax.ppermute(sent, 'tm', [(i_2, i_2 ^ lap) for i_2 in range(count)])  5.94 us
    dot_general x1, matrix products, fine_section(): jnp.matmul(summed[1], cosine_table, precision=highest)  5.05 us
    dot_general x1, matrix products, fine_section(): jnp.matmul(summed[0], cosine_table, precision=highest)  4.87 us
    dot_general x1, matrix products, fine_section(): jnp.matmul(summed[1], sine_table, precision=highest)  4.86 us
    dot_general x1, matrix products, fine_section(): jnp.matmul(summed[0], sine_table, precision=highest)  4.86 us
    ppermute x3, starting transfers between devices, on_device(): lax.ppermute(sent, 'tm', [(i_2, i_2 ^ lap) for i_2 in range(count)])  4.12 us
    ppermute x1, starting transfers between devices, from_behind(): return lax.ppermute(array, axis, pairs)  2.39 us
  transfers between devices with their start and end apart: 4, of which 2 were waited for; matrix products, arithmetic and copies ran while one was open for 7% of the time, Pallas kernels for 0%

profile of v1, /device:TPU:0, one launch (start us, length us, event | category | flops | bytes accessed | tf_op | source)
XLA Modules:
  0.0 51.9 jit_solution(1405505108227669346)
XLA Ops:
  0.0 0.8 %slice.180 = f32[2,960]{1,0:T(2,128)S(1)} slice(f32[2,65536]{1,0:T(2,128)} %param.3), slice={[0:2], [64576:65536]} | slice | bytes 15360 | tf_op jit(solution)/shard_map/slice | solution.py:88
  0.8 2.4 %collective-permute-start = (f32[2,960]{1,0:T(2,128)S(1)}, f32[2,960]{1,0:T(2,128)S(1)}, u32[]{:S(2)}, u32[]{:S(2)}) collective-permute-start(f32[2,960]{1,0:T(2,128)S(1)} %slice.180), channel_id=1, source_target_pairs={{0,1},{1,2},{2,3},{4,5},{5,6},{6,7},{8,9},{9,10},{10,11},{12,13},{... | collective-permute-start | bytes 23048 | tf_op jit(solution)/shard_map/ppermute | solution.py:27
  3.2 1.0 %fusion.142 = (f32[1,512]{1,0:T(1,128)S(1)}, f32[1,512]{1,0:T(1,128)S(1)}, f32[1,512]{1,0:T(1,128)S(1)}, f32[1,512]{1,0:T(1,128)S(1)}, f32[1,512]{1,0:T(1,128)S(...) fusion(f32[12,512]{1,0:T(8,128)} %param.5), kind=kLoop, calls=%fused_computation.217 | loop fusion | flops 2048 | bytes 49152 | tf_op jit(solution)/shard_map/slice | solution.py:69
  4.2 1.0 %slice_bitcast_fusion.21 = (f32[64]{0:T(128)S(1)}, f32[64]{0:T(128)S(1)}, f32[64]{0:T(128)S(1)}, f32[64]{0:T(128)S(1)}, f32[64]{0:T(128)S(1)}, /*index=5*/f32[64...) fusion(f32[16,64]{1,0:T(8,128)} %param.4), kind=kLoop, calls=%fused_computation.191 | loop fusion | bytes 8192 | tf_op jit(solution)/shard_map/tile | solution.py:43
  6.7 4.7 %fusion.21 = (f32[1,2,512,128]{3,1,2,0:T(2,128)S(1)}, f32[1,2,512,128]{3,1,2,0:T(2,128)S(1)}, f32[1,2,512,128]{3,1,2,0:T(2,128)S(1)}, f32[1,2,512,128]{3,1,2,0:T...) fusion(f32[2,960]{1,0:T(2,128)S(1)} %collective-permute-done, f32[2,65536]{1,0:T(2,128)} %param.3), kind=kLoop, calls=%fused_computation.58 | loop fusion | flops 786432 | bytes 3677696
  11.3 2.6 %fusion.33 = (f32[1,2,512,128]{3,1,2,0:T(2,128)S(1)}, f32[1,2,512,128]{3,1,2,0:T(2,128)S(1)}, f32[1,2,512,128]{3,1,2,0:T(2,128)S(1)}, f32[1,2,512,128]{3,1,2,0:T...) fusion(f32[2,960]{1,0:T(2,128)S(1)} %collective-permute-done, f32[2,65536]{1,0:T(2,128)S(1)} %copy-done), kind=kLoop, calls=%fused_computation.70 | loop fusion | flops 786432 | bytes 3677696
  13.9 1.3 %fusion.45 = (f32[1,2,512,128]{3,1,2,0:T(2,128)S(1)}, f32[1,2,512,128]{3,1,2,0:T(2,128)S(1)}, f32[1,2,512,128]{3,1,2,0:T(2,128)S(1)}) fusion(f32[2,960]{1,0:T(2,128)S(1)} %collective-permute-done, f32[2,65536]{1,0:T(2,128)S(1)} %copy-done), kind=kLoop, calls=%fused_computation.82 | loop fusion | flops 393216 | bytes 2104832
  15.2 0.6 %fusion.64 = f32[2,512,128]{2,1,0:T(8,128)S(1)} fusion(f32[1,2,512,128]{3,1,2,0:T(2,128)S(1)} %get-tuple-element.18, f32[1,2,512,128]{3,1,2,0:T(2,128)S(1)} %get-tuple-element.19, f32[1,2,512,128]{3,1,2,0:T(2,128)S(1)} %get-tuple-element.17, f32[1,2,512,128]{3,1,2,0:T(2,128)S(1)} %get-tuple-element.16, f32[1,2,512,128]{3,1,2,0:T(2,128)S(1)} %get-tuple-element.15, ...), kind=kLoop, calls=%fused_computation.102 | loop fusion | flops 4063232 | bytes 8921088 | tf_op jit(solution)/shard_map/add | solution.py:43
  16.0 0.8 %fusion.102 = f32[64,1024]{1,0:T(8,128)S(1)} fusion(f32[1024,64]{1,0:T(8,128)S(1)} %squeeze.26), kind=kOutput, calls=%fused_computation.159 | convolution fusion | flops 50388992 | bytes 524288 | tf_op jit(solution)/shard_map/kp,tp->kt/dot_general | solution.py:55
  17.0 0.8 %fusion.104 = f32[64,1024]{1,0:T(8,128)S(1)} fusion(f32[1024,64]{1,0:T(8,128)S(1)} %squeeze.25), kind=kOutput, calls=%fused_computation.160 | convolution fusion | flops 50388992 | bytes 524288 | tf_op jit(solution)/shard_map/kp,tp->kt/dot_general | solution.py:51
  17.8 0.8 %fusion = f32[64,1024]{1,0:T(8,128)S(1)} fusion(f32[64,1024]{1,0:T(8,128)S(1)} %fusion.102, f32[1024,64]{1,0:T(8,128)S(1)} %squeeze.25), kind=kOutput, calls=%fused_computation.26 | convolution fusion | flops 50520064 | bytes 786432 | tf_op jit(solution)/shard_map/kp,tp->kt/dot_general | solution.py:56
  18.6 0.8 %fusion.1 = f32[64,1024]{1,0:T(8,128)S(1)} fusion(f32[64,1024]{1,0:T(8,128)S(1)} %fusion.104, f32[1024,64]{1,0:T(8,128)S(1)} %squeeze.26), kind=kOutput, calls=%fused_computation.28 | convolution fusion | flops 50520064 | bytes 786432 | tf_op jit(solution)/shard_map/kp,tp->kt/dot_general | solution.py:52
  19.5 2.7 %collective-permute-start.1 = (f32[2,16,1024]{2,1,0:T(8,128)S(1)}, f32[2,16,1024]{2,1,0:T(8,128)S(1)}, u32[]{:S(2)}, u32[]{:S(2)}) collective-permute-start(f32[2,16,1024]{2,1,0:T(8,128)S(1)} %get-tuple-element.21), channel_id=1, source_target_pairs={{0,1},{1,0},{2,3},{3,2},{4,5},{5,4},{6,7},{7,6},{8,9},{9,8},{10,11... | collective-permute-start | bytes 393224 | tf_op jit(solution)/shard_map/ppermute | solution.py:97
  22.2 1.4 %collective-permute-start.3 = (f32[2,16,1024]{2,1,0:T(8,128)S(1)}, f32[2,16,1024]{2,1,0:T(8,128)S(1)}, u32[]{:S(2)}, u32[]{:S(2)}) collective-permute-start(f32[2,16,1024]{2,1,0:T(8,128)S(1)} %get-tuple-element.23), channel_id=1, source_target_pairs={{0,3},{1,2},{2,1},{3,0},{4,7},{5,6},{6,5},{7,4},{8,11},{9,10},{10,... | collective-permute-start | bytes 393224 | tf_op jit(solution)/shard_map/ppermute | solution.py:97
  23.6 4.9 %collective-permute-done.2 = f32[2,16,1024]{2,1,0:T(8,128)S(1)} collective-permute-done((f32[2,16,1024]{2,1,0:T(8,128)S(1)}, f32[2,16,1024]{2,1,0:T(8,128)S(1)}, u32[]{:S(2)}, u32[]{:S(2)}) %collective-permute-start.2) | collective-permute-done | bytes 131104 | tf_op jit(solution)/shard_map/ppermute | solution.py:97
  28.5 1.0 %collective-permute-done.3 = f32[2,16,1024]{2,1,0:T(8,128)S(1)} collective-permute-done((f32[2,16,1024]{2,1,0:T(8,128)S(1)}, f32[2,16,1024]{2,1,0:T(8,128)S(1)}, u32[]{:S(2)}, u32[]{:S(2)}) %collective-permute-start.3) | collective-permute-done | bytes 131104 | tf_op jit(solution)/shard_map/ppermute | solution.py:97
  29.6 0.6 %gather_fusion = f32[4,2,16,1024]{3,2,1,0:T(8,128)S(1)} fusion(f32[4,2,16,1024]{3,2,1,0:T(8,128)S(1)} %pad_maximum_fusion.1, s32[1024]{0:T(1024)S(1)} %pad_clamp_fusion), kind=kCustom, calls=%fused_computation | custom fusion | bytes 1048592 | tf_op jit(solution)/shard_map/gather | solution.py:98
  30.2 0.3 copy.4
  30.8 0.6 %fusion.57 = f32[2,16,8,512]{3,2,1,0:T(8,128)S(1)} fusion(f32[2,16,8,512]{3,2,1,0:T(8,128)S(1)} %reshape_reshape.3, f32[512]{0:T(512)S(1)} %bitcast.226, f32[512]{0:T(512)S(1)} %bitcast.227, f32[512]{0:T(512)S(1)} %bitcast.217, f32[512]{0:T(512)S(1)} %bitcast.218, f32[512]{0:T(512)S(1)} %bitcast.219, f32[512]{0:T(512)S(1)} %bitcast.220, ...), kind=kLoop, calls=%fused_computation.94 | loop fusion | flops 2490368 | bytes 1073152 | tf_op jit(solution)/shard_map/add | solution.py:69
  31.3 4.9 %fusion.13 = f32[16,8,512]{2,1,0:T(8,128)S(1)} fusion(f32[2,16,8,512]{3,2,1,0:T(8,128)S(1)} %fusion.57), kind=kOutput, calls=%fused_computation.42 | convolution fusion | flops 406323200 | bytes 524288 | tf_op jit(solution)/shard_map/dot_general | solution.py:74
  36.2 5.1 %fusion.11 = f32[16,8,512]{2,1,0:T(8,128)S(1)} fusion(f32[2,16,8,512]{3,2,1,0:T(8,128)S(1)} %fusion.57), kind=kOutput, calls=%fused_computation.40 | convolution fusion | flops 406323200 | bytes 524288 | tf_op jit(solution)/shard_map/dot_general | solution.py:78
  41.3 4.9 %fusion.5 = f32[1,16,8,512]{3,2,1,0:T(8,128)S(1)} fusion(f32[16,8,512]{2,1,0:T(8,128)S(1)} %fusion.13, f32[2,16,8,512]{3,2,1,0:T(8,128)S(1)} %fusion.57), kind=kOutput, calls=%fused_computation.34 | convolution fusion | flops 406454272 | bytes 786432 | tf_op jit(solution)/shard_map/dot_general | solution.py:75
  46.2 4.9 %fusion.3 = f32[1,16,8,512]{3,2,1,0:T(8,128)S(1)} fusion(f32[16,8,512]{2,1,0:T(8,128)S(1)} %fusion.11, f32[2,16,8,512]{3,2,1,0:T(8,128)S(1)} %fusion.57), kind=kOutput, calls=%fused_computation.31 | convolution fusion | flops 406454272 | bytes 786432 | tf_op jit(solution)/shard_map/dot_general | solution.py:79
  51.0 0.8 %pad_maximum_fusion.2 = f32[2,16,8,512]{3,2,1,0:T(8,128)} fusion(f32[1,16,8,512]{3,2,1,0:T(8,128)S(1)} %fusion.3, f32[1,16,8,512]{3,2,1,0:T(8,128)S(1)} %fusion.5), kind=kLoop, calls=%fused_computation.135 | loop fusion | flops 131072 | bytes 1048576 | tf_op jit(solution)/shard_map/stack | solution.py:81
  (45 shorter events, 2.0 us)
Async XLA Ops:
  0.8 5.9 %collective-permute-start = (f32[2,960]{1,0:T(2,128)S(1)}, f32[2,960]{1,0:T(2,128)S(1)}, u32[]{:S(2)}, u32[]{:S(2)}) collective-permute-start(f32[2,960]{1,0:T(2,128)S(1)} %slice.180), channel_id=1, source_target_pairs={{0,1},{1,2},{2,3},{4,5},{5,6},{6,7},{8,9},{9,10},{10,11},{12,13},{... | collective-permute-start | bytes 23048 | tf_op jit(solution)/shard_map/ppermute | solution.py:27
  6.7 4.7 %copy-start = (f32[2,65536]{1,0:T(2,128)S(1)}, f32[2,65536]{1,0:T(2,128)}, u32[]{:S(2)}) copy-start(f32[2,65536]{1,0:T(2,128)} %param.3) | copy-start | bytes 1572868
  19.5 4.1 %collective-permute-start.1 = (f32[2,16,1024]{2,1,0:T(8,128)S(1)}, f32[2,16,1024]{2,1,0:T(8,128)S(1)}, u32[]{:S(2)}, u32[]{:S(2)}) collective-permute-start(f32[2,16,1024]{2,1,0:T(8,128)S(1)} %get-tuple-element.21), channel_id=1, source_target_pairs={{0,1},{1,0},{2,3},{3,2},{4,5},{5,4},{6,7},{7,6},{8,9},{9,8},{10,11... | collective-permute-start | bytes 393224 | tf_op jit(solution)/shard_map/ppermute | solution.py:97
  22.2 6.4 %collective-permute-start.2 = (f32[2,16,1024]{2,1,0:T(8,128)S(1)}, f32[2,16,1024]{2,1,0:T(8,128)S(1)}, u32[]{:S(2)}, u32[]{:S(2)}) collective-permute-start(f32[2,16,1024]{2,1,0:T(8,128)S(1)} %get-tuple-element.22), channel_id=1, source_target_pairs={{0,2},{1,3},{2,0},{3,1},{4,6},{5,7},{6,4},{7,5},{8,10},{9,11},{10,... | collective-permute-start | bytes 393224 | tf_op jit(solution)/shard_map/ppermute | solution.py:97
  22.2 7.4 %collective-permute-start.3 = (f32[2,16,1024]{2,1,0:T(8,128)S(1)}, f32[2,16,1024]{2,1,0:T(8,128)S(1)}, u32[]{:S(2)}, u32[]{:S(2)}) collective-permute-start(f32[2,16,1024]{2,1,0:T(8,128)S(1)} %get-tuple-element.23), channel_id=1, source_target_pairs={{0,3},{1,2},{2,1},{3,0},{4,7},{5,6},{6,5},{7,4},{8,11},{9,10},{10,... | collective-permute-start | bytes 393224 | tf_op jit(solution)/shard_map/ppermute | solution.py:97
